TPU v7x, 768 devices: a whole 4x8x12 slice. The times are simulated.
768 devices in a mesh: mem: 32 (over y, x_hi, core), tile: 24 (over z, x_lo).
Axes of the slice: x: 4 (x_hi: 2, x_lo: 2; x = x_hi * 2 + x_lo), y: 8, z: 12, core: 2. Of those that a mesh axis runs over, the one named last changes fastest.
Arguments:
- alpha_fields: float32 [96, 768, 768], P('mem', 'tile'), may hold values from -6 to 6
- static_control: float32 [4, 768, 768], P(None, 'tile'), as said below
- perturbations: bfloat16 [96, 4, 768, 768], P('mem', None, 'tile'), may hold values from -6 to 6
- coef_table: float32 [8], replicated, may hold values from 0.12 to 0.25
- coef_class: int32 [768, 768], P('tile'), may hold values from 0 to 7
- obs_cells: int32 [24, 4096], P('tile'), may hold values from 0 to 98303
- obs_counts: int32 [24], P('tile'), may hold values from 2048 to 4096, as said below
- innovations: float32 [24, 4096], P('tile'), as said below
- obs_weights: float32 [24, 4096], P('tile'), may hold values from 10 to 100
Outputs:
- grad_alpha: float32 [96, 768, 768], P('mem', 'tile')
- grad_static: float32 [4, 768, 768], P(None, 'tile')
Inputs may be any that keep to these rules, and one draw needn't show every extreme that they name: `obs_counts`: at most 4096, and some strip uses all 4096 slots in every draw. `static_control`: real values. `innovations`: real values.
All inputs are finite; a program needn't handle non-finite values.
Results may differ from a plain program's by a relative error of at most 0.0004.
Values sent between devices are 32-bit elements; how exact they have to be, the bound alone decides.
A program may use at most 32 MiB of HBM per device.

v0:
```python
import jax
import jax.numpy as jnp
from jax import lax
from jax.sharding import PartitionSpec as P

STEPS = 4


def with_halo(cells, sides, width):
    for axis, dim in sides:
        count = lax.axis_size(axis)
        ends = count - 1
        head = lax.slice_in_dim(cells, 0, width, axis=dim)
        tail = lax.slice_in_dim(cells, cells.shape[dim] - width, cells.shape[dim], axis=dim)
        cells = jnp.concatenate(
            [
                lax.ppermute(tail, axis, [(i, (i + 1) % count) for i in range(ends)]),
                cells,
                lax.ppermute(head, axis, [((i + 1) % count, i) for i in range(ends)]),
            ],
            axis=dim,
        )
    return cells


def lookup(coef_table, classes):
    one_hot = (
        classes[None] == jnp.arange(coef_table.shape[0], dtype=jnp.int32)[:, None, None]
    ).astype(jnp.float32)
    return jnp.sum(one_hot * coef_table[:, None, None], axis=0)


def beside_all(padded):
    return padded[:, 2:, 1:-1] + padded[:, :-2, 1:-1] + padded[:, 1:-1, 2:] + padded[:, 1:-1, :-2]


def pad_cols(field):
    return jnp.pad(field, ((0, 0), (0, 0), (1, 1)))


def body(
    alpha_fields,
    static_control,
    perturbations,
    coef_table,
    coef_class,
    obs_cells,
    obs_counts,
    innovations,
    obs_weights,
):
    kappa = lookup(coef_table, coef_class)
    owned = alpha_fields.shape[0]
    ens_scale = (owned * lax.axis_size("mem") - 1.0) ** (-0.5)
    fields = jnp.concatenate([alpha_fields, static_control], 0)
    current = fields
    for step in range(STEPS):
        padded = pad_cols(with_halo(current, (("tile", 1),), 1))
        current = current + kappa * (beside_all(padded) - 4.0 * current)
    moved_alpha = current[:owned]
    moved_static = current[owned:]
    partial_value = ens_scale * jnp.sum(perturbations * moved_alpha[:, None], 0)
    counted = jnp.arange(obs_cells.shape[1], dtype=jnp.int32) < obs_counts[0]
    cells_here = obs_cells[0]
    picked = partial_value.reshape(-1)[cells_here]
    summed = lax.psum(picked, "mem")
    observed = summed + moved_static.reshape(-1)[cells_here]
    residual = jnp.where(counted, (observed - innovations[0]) * obs_weights[0], 0.0)
    forcing = (
        jnp.zeros((moved_static.size,), jnp.float32)
        .at[cells_here]
        .add(residual)
        .reshape(moved_static.shape)
    )
    member_adj = ens_scale * jnp.sum(perturbations * forcing[None], 1)
    adjoint = jnp.concatenate([member_adj, forcing], 0)
    current = adjoint
    for step in range(STEPS):
        weighted = kappa * current
        padded = pad_cols(with_halo(weighted, (("tile", 1),), 1))
        current = current + (beside_all(padded) - 4.0 * weighted)
    grads = fields + current
    return (grads[:owned], grads[owned:])


def solution(mesh):
    in_specs = (
        P("mem", "tile", None),
        P(None, "tile", None),
        P("mem", None, "tile", None),
        P(),
        P("tile", None),
        P("tile", None),
        P("tile"),
        P("tile", None),
        P("tile", None),
    )
    out_specs = (P("mem", "tile", None), P(None, "tile", None))
    return jax.shard_map(body, mesh=mesh, in_specs=in_specs, out_specs=out_specs, check_vma=False)
```

profile of v0, /device:TPU:130, one launch (start us, length us, event | category | flops | bytes accessed | tf_op | source)
XLA Modules:
  0.0 293.8 jit_solution(15882616223816209855)
XLA Ops:
  0.6 1.0 constant_dynamic-update-slice_fusion.1
  1.7 1.0 constant_dynamic-update-slice_fusion
  2.7 4.3 %collective-permute-start.1 = (f32[7,1,768]{2,1,0:T(1,128)S(1)}, f32[7,1,768]{2,1,0:T(1,128)S(1)}, u32[]{:S(2)}, u32[]{:S(2)}) collective-permute-start(f32[7,1,768]{2,1,0:T(1,128)S(1)} %get-tuple-element.22), channel_id=1, source_target_pairs={{0,1},{1,2},{2,3},{3,4},{4,5},{5,6},{6,7},{7,8},{8,9},{9,10},{10,1... | collective-permute-start | bytes 64520 | tf_op jit(solution)/shard_map/ppermute | solution.py:17
  7.0 1.9 collective-permute-start
  9.1 4.5 %collective-permute-done = f32[7,1,768]{2,1,0:T(1,128)S(1)} collective-permute-done((f32[7,1,768]{2,1,0:T(1,128)S(1)}, f32[7,1,768]{2,1,0:T(1,128)S(1)}, u32[]{:S(2)}, u32[]{:S(2)}) %collective-permute-start) | collective-permute-done | bytes 21536 | tf_op jit(solution)/shard_map/ppermute | solution.py:19
  14.6 4.0 %collective-permute-start.3 = (f32[7,1,768]{2,1,0:T(1,128)S(1)}, f32[7,1,768]{2,1,0:T(1,128)S(1)}, u32[]{:S(2)}, u32[]{:S(2)}) collective-permute-start(f32[7,1,768]{2,1,0:T(1,128)S(1)} %get-tuple-element.20), channel_id=1, source_target_pairs={{0,1},{1,2},{2,3},{3,4},{4,5},{5,6},{6,7},{7,8},{8,9},{9,10},{10,1... | collective-permute-start | bytes 64520 | tf_op jit(solution)/shard_map/ppermute | solution.py:17
  18.6 1.9 collective-permute-start.2
  20.6 5.9 %collective-permute-done.2 = f32[7,1,768]{2,1,0:T(1,128)S(1)} collective-permute-done((f32[7,1,768]{2,1,0:T(1,128)S(1)}, f32[7,1,768]{2,1,0:T(1,128)S(1)}, u32[]{:S(2)}, u32[]{:S(2)}) %collective-permute-start.2) | collective-permute-done | bytes 21536 | tf_op jit(solution)/shard_map/ppermute | solution.py:19
  27.4 3.9 %collective-permute-start.5 = (f32[7,1,768]{2,1,0:T(1,128)S(1)}, f32[7,1,768]{2,1,0:T(1,128)S(1)}, u32[]{:S(2)}, u32[]{:S(2)}) collective-permute-start(f32[7,1,768]{2,1,0:T(1,128)S(1)} %get-tuple-element.18), channel_id=1, source_target_pairs={{0,1},{1,2},{2,3},{3,4},{4,5},{5,6},{6,7},{7,8},{8,9},{9,10},{10,1... | collective-permute-start | bytes 64520 | tf_op jit(solution)/shard_map/ppermute | solution.py:17
  31.3 1.9 collective-permute-start.4
  33.3 4.6 %collective-permute-done.4 = f32[7,1,768]{2,1,0:T(1,128)S(1)} collective-permute-done((f32[7,1,768]{2,1,0:T(1,128)S(1)}, f32[7,1,768]{2,1,0:T(1,128)S(1)}, u32[]{:S(2)}, u32[]{:S(2)}) %collective-permute-start.4) | collective-permute-done | bytes 21536 | tf_op jit(solution)/shard_map/ppermute | solution.py:19
  38.9 3.1 %collective-permute-start.7 = (f32[7,1,768]{2,1,0:T(1,128)S(1)}, f32[7,1,768]{2,1,0:T(1,128)S(1)}, u32[]{:S(2)}, u32[]{:S(2)}) collective-permute-start(f32[7,1,768]{2,1,0:T(1,128)S(1)} %get-tuple-element.16), channel_id=1, source_target_pairs={{0,1},{1,2},{2,3},{3,4},{4,5},{5,6},{6,7},{7,8},{8,9},{9,10},{10,1... | collective-permute-start | bytes 64520 | tf_op jit(solution)/shard_map/ppermute | solution.py:17
  42.0 2.7 collective-permute-start.6
  45.4 3.2 %collective-permute-done.6 = f32[7,1,768]{2,1,0:T(1,128)S(1)} collective-permute-done((f32[7,1,768]{2,1,0:T(1,128)S(1)}, f32[7,1,768]{2,1,0:T(1,128)S(1)}, u32[]{:S(2)}, u32[]{:S(2)}) %collective-permute-start.6) | collective-permute-done | bytes 21536 | tf_op jit(solution)/shard_map/ppermute | solution.py:19
  49.7 1.0 copy-done
  50.8 23.0 %gather_fusion.1 = f32[4096]{0:T(1024)S(1)} fusion(f32[98304]{0:T(1024)S(1)} %reshape.45, s32[4096]{0:T(1024)S(1)} %broadcast_clamp_fusion), kind=kCustom, calls=%fused_computation.1 | custom fusion | bytes 49152 | tf_op jit(solution)/shard_map/gather | solution.py:67
  73.9 23.0 %gather_fusion = f32[4096]{0:T(1024)S(1)} fusion(f32[98304]{0:T(1024)S(1)} %mul.134, s32[4096]{0:T(1024)S(1)} %broadcast_clamp_fusion), kind=kCustom, calls=%fused_computation | custom fusion | bytes 49152 | tf_op jit(solution)/shard_map/gather | solution.py:65
  96.9 128.6 %psum.7 = f32[4096]{0:T(1024)S(1)} all-reduce(f32[4096]{0:T(1024)S(1)} %gather_fusion), channel_id=1, replica_groups=mesh['mem'=32,'tile'=24] {'mem'}, use_global_device_ids=true, to_apply=%region_2.3 | all-reduce | flops 4096 | bytes 32768 | tf_op jit(solution)/shard_map/psum | solution.py:66
  225.5 22.0 %scatter_custom_fusion = f32[98304]{0:T(1024)S(1)} fusion(s32[4096]{0:T(1024)S(1)} %bitcast.8, f32[4096]{0:T(1024)S(1)} %multiply_select_fusion, f32[]{:T(128)} %constant.5.clone.1), kind=kCustom, calls=%fused_computation.95 | custom fusion | flops 4096 | bytes 393220 | tf_op jit(solution)/shard_map/scatter-add | solution.py:72
  247.8 4.2 %collective-permute-start.9 = (f32[7,1,768]{2,1,0:T(1,128)S(1)}, f32[7,1,768]{2,1,0:T(1,128)S(1)}, u32[]{:S(2)}, u32[]{:S(2)}) collective-permute-start(f32[7,1,768]{2,1,0:T(1,128)S(1)} %get-tuple-element.14), channel_id=1, source_target_pairs={{0,1},{1,2},{2,3},{3,4},{4,5},{5,6},{6,7},{7,8},{8,9},{9,10},{10,1... | collective-permute-start | bytes 64520 | tf_op jit(solution)/shard_map/ppermute | solution.py:17
  252.1 1.9 collective-permute-start.8
  254.0 4.6 %collective-permute-done.8 = f32[7,1,768]{2,1,0:T(1,128)S(1)} collective-permute-done((f32[7,1,768]{2,1,0:T(1,128)S(1)}, f32[7,1,768]{2,1,0:T(1,128)S(1)}, u32[]{:S(2)}, u32[]{:S(2)}) %collective-permute-start.8) | collective-permute-done | bytes 21536 | tf_op jit(solution)/shard_map/ppermute | solution.py:19
  259.7 2.5 collective-permute-start.11
  262.2 3.3 %collective-permute-start.10 = (f32[7,1,768]{2,1,0:T(1,128)S(1)}, f32[7,1,768]{2,1,0:T(1,128)S(1)}, u32[]{:S(2)}, u32[]{:S(2)}) collective-permute-start(f32[7,1,768]{2,1,0:T(1,128)S(1)} %get-tuple-element.13), channel_id=1, source_target_pairs={{1,0},{2,1},{3,2},{4,3},{5,4},{6,5},{7,6},{8,7},{9,8},{10,9},{11,1... | collective-permute-start | bytes 64520 | tf_op jit(solution)/shard_map/ppermute | solution.py:19
  265.5 3.6 %collective-permute-done.10 = f32[7,1,768]{2,1,0:T(1,128)S(1)} collective-permute-done((f32[7,1,768]{2,1,0:T(1,128)S(1)}, f32[7,1,768]{2,1,0:T(1,128)S(1)}, u32[]{:S(2)}, u32[]{:S(2)}) %collective-permute-start.10) | collective-permute-done | bytes 21536 | tf_op jit(solution)/shard_map/ppermute | solution.py:19
  270.1 3.9 %collective-permute-start.13 = (f32[7,1,768]{2,1,0:T(1,128)S(1)}, f32[7,1,768]{2,1,0:T(1,128)S(1)}, u32[]{:S(2)}, u32[]{:S(2)}) collective-permute-start(f32[7,1,768]{2,1,0:T(1,128)S(1)} %get-tuple-element.10), channel_id=1, source_target_pairs={{0,1},{1,2},{2,3},{3,4},{4,5},{5,6},{6,7},{7,8},{8,9},{9,10},{10,1... | collective-permute-start | bytes 64520 | tf_op jit(solution)/shard_map/ppermute | solution.py:17
  274.0 1.9 collective-permute-start.12
  275.9 4.9 %collective-permute-done.12 = f32[7,1,768]{2,1,0:T(1,128)S(1)} collective-permute-done((f32[7,1,768]{2,1,0:T(1,128)S(1)}, f32[7,1,768]{2,1,0:T(1,128)S(1)}, u32[]{:S(2)}, u32[]{:S(2)}) %collective-permute-start.12) | collective-permute-done | bytes 21536 | tf_op jit(solution)/shard_map/ppermute | solution.py:19
  281.8 2.9 collective-permute-start.15
  284.7 2.9 collective-permute-start.14
  287.7 3.7 %collective-permute-done.14 = f32[7,1,768]{2,1,0:T(1,128)S(1)} collective-permute-done((f32[7,1,768]{2,1,0:T(1,128)S(1)}, f32[7,1,768]{2,1,0:T(1,128)S(1)}, u32[]{:S(2)}, u32[]{:S(2)}) %collective-permute-start.14) | collective-permute-done | bytes 21536 | tf_op jit(solution)/shard_map/ppermute | solution.py:19
  293.0 0.8 slice.279
  (58 shorter events, 9.2 us)
Async XLA Ops:
  0.6 8.3 %copy-start.1 = (s32[32,768]{1,0:T(8,128)S(1)}, s32[32,768]{1,0:T(8,128)}, u32[]{:S(2)}) copy-start(s32[32,768]{1,0:T(8,128)} %param.13) | copy-start | bytes 294916
  0.6 8.3 %copy-start.5 = (f32[8]{0:T(128)S(1)}, f32[8]{0:T(128)}, u32[]{:S(2)}) copy-start(f32[8]{0:T(128)} %param.12) | copy-start | bytes 100
  2.7 6.4 %collective-permute-start.1 = (f32[7,1,768]{2,1,0:T(1,128)S(1)}, f32[7,1,768]{2,1,0:T(1,128)S(1)}, u32[]{:S(2)}, u32[]{:S(2)}) collective-permute-start(f32[7,1,768]{2,1,0:T(1,128)S(1)} %get-tuple-element.22), channel_id=1, source_target_pairs={{0,1},{1,2},{2,3},{3,4},{4,5},{5,6},{6,7},{7,8},{8,9},{9,10},{10,1... | collective-permute-start | bytes 64520 | tf_op jit(solution)/shard_map/ppermute | solution.py:17
  7.0 6.6 %collective-permute-start = (f32[7,1,768]{2,1,0:T(1,128)S(1)}, f32[7,1,768]{2,1,0:T(1,128)S(1)}, u32[]{:S(2)}, u32[]{:S(2)}) collective-permute-start(f32[7,1,768]{2,1,0:T(1,128)S(1)} %get-tuple-element.23), channel_id=1, source_target_pairs={{1,0},{2,1},{3,2},{4,3},{5,4},{6,5},{7,6},{8,7},{9,8},{10,9},{11,1... | collective-permute-start | bytes 64520 | tf_op jit(solution)/shard_map/ppermute | solution.py:19
  14.6 6.0 %collective-permute-start.3 = (f32[7,1,768]{2,1,0:T(1,128)S(1)}, f32[7,1,768]{2,1,0:T(1,128)S(1)}, u32[]{:S(2)}, u32[]{:S(2)}) collective-permute-start(f32[7,1,768]{2,1,0:T(1,128)S(1)} %get-tuple-element.20), channel_id=1, source_target_pairs={{0,1},{1,2},{2,3},{3,4},{4,5},{5,6},{6,7},{7,8},{8,9},{9,10},{10,1... | collective-permute-start | bytes 64520 | tf_op jit(solution)/shard_map/ppermute | solution.py:17
  18.6 7.8 %collective-permute-start.2 = (f32[7,1,768]{2,1,0:T(1,128)S(1)}, f32[7,1,768]{2,1,0:T(1,128)S(1)}, u32[]{:S(2)}, u32[]{:S(2)}) collective-permute-start(f32[7,1,768]{2,1,0:T(1,128)S(1)} %get-tuple-element.21), channel_id=1, source_target_pairs={{1,0},{2,1},{3,2},{4,3},{5,4},{6,5},{7,6},{8,7},{9,8},{10,9},{11,1... | collective-permute-start | bytes 64520 | tf_op jit(solution)/shard_map/ppermute | solution.py:19
  26.9 6.4 %copy-start.4 = (s32[1,4096]{1,0:T(1,128)S(1)}, s32[1,4096]{1,0:T(1,128)}, u32[]{:S(2)}) copy-start(s32[1,4096]{1,0:T(1,128)} %param.14) | copy-start | bytes 49156
  27.4 5.9 %collective-permute-start.5 = (f32[7,1,768]{2,1,0:T(1,128)S(1)}, f32[7,1,768]{2,1,0:T(1,128)S(1)}, u32[]{:S(2)}, u32[]{:S(2)}) collective-permute-start(f32[7,1,768]{2,1,0:T(1,128)S(1)} %get-tuple-element.18), channel_id=1, source_target_pairs={{0,1},{1,2},{2,3},{3,4},{4,5},{5,6},{6,7},{7,8},{8,9},{9,10},{10,1... | collective-permute-start | bytes 64520 | tf_op jit(solution)/shard_map/ppermute | solution.py:17
  31.3 6.6 %collective-permute-start.4 = (f32[7,1,768]{2,1,0:T(1,128)S(1)}, f32[7,1,768]{2,1,0:T(1,128)S(1)}, u32[]{:S(2)}, u32[]{:S(2)}) collective-permute-start(f32[7,1,768]{2,1,0:T(1,128)S(1)} %get-tuple-element.19), channel_id=1, source_target_pairs={{1,0},{2,1},{3,2},{4,3},{5,4},{6,5},{7,6},{8,7},{9,8},{10,9},{11,1... | collective-permute-start | bytes 64520 | tf_op jit(solution)/shard_map/ppermute | solution.py:19
  38.9 6.5 %collective-permute-start.7 = (f32[7,1,768]{2,1,0:T(1,128)S(1)}, f32[7,1,768]{2,1,0:T(1,128)S(1)}, u32[]{:S(2)}, u32[]{:S(2)}) collective-permute-start(f32[7,1,768]{2,1,0:T(1,128)S(1)} %get-tuple-element.16), channel_id=1, source_target_pairs={{0,1},{1,2},{2,3},{3,4},{4,5},{5,6},{6,7},{7,8},{8,9},{9,10},{10,1... | collective-permute-start | bytes 64520 | tf_op jit(solution)/shard_map/ppermute | solution.py:17
  42.0 6.6 %collective-permute-start.6 = (f32[7,1,768]{2,1,0:T(1,128)S(1)}, f32[7,1,768]{2,1,0:T(1,128)S(1)}, u32[]{:S(2)}, u32[]{:S(2)}) collective-permute-start(f32[7,1,768]{2,1,0:T(1,128)S(1)} %get-tuple-element.17), channel_id=1, source_target_pairs={{1,0},{2,1},{3,2},{4,3},{5,4},{6,5},{7,6},{8,7},{9,8},{10,9},{11,1... | collective-permute-start | bytes 64520 | tf_op jit(solution)/shard_map/ppermute | solution.py:19
  49.5 1.1 copy-start
  73.9 151.6 %copy-start.2 = (f32[1,4096]{1,0:T(1,128)S(1)}, f32[1,4096]{1,0:T(1,128)}, u32[]{:S(2)}) copy-start(f32[1,4096]{1,0:T(1,128)} %param.17) | copy-start | bytes 49156
  73.9 151.6 %copy-start.3 = (f32[1,4096]{1,0:T(1,128)S(1)}, f32[1,4096]{1,0:T(1,128)}, u32[]{:S(2)}) copy-start(f32[1,4096]{1,0:T(1,128)} %param.16) | copy-start | bytes 49156
  247.8 6.2 %collective-permute-start.9 = (f32[7,1,768]{2,1,0:T(1,128)S(1)}, f32[7,1,768]{2,1,0:T(1,128)S(1)}, u32[]{:S(2)}, u32[]{:S(2)}) collective-permute-start(f32[7,1,768]{2,1,0:T(1,128)S(1)} %get-tuple-element.14), channel_id=1, source_target_pairs={{0,1},{1,2},{2,3},{3,4},{4,5},{5,6},{6,7},{7,8},{8,9},{9,10},{10,1... | collective-permute-start | bytes 64520 | tf_op jit(solution)/shard_map/ppermute | solution.py:17
  252.1 6.6 %collective-permute-start.8 = (f32[7,1,768]{2,1,0:T(1,128)S(1)}, f32[7,1,768]{2,1,0:T(1,128)S(1)}, u32[]{:S(2)}, u32[]{:S(2)}) collective-permute-start(f32[7,1,768]{2,1,0:T(1,128)S(1)} %get-tuple-element.15), channel_id=1, source_target_pairs={{1,0},{2,1},{3,2},{4,3},{5,4},{6,5},{7,6},{8,7},{9,8},{10,9},{11,1... | collective-permute-start | bytes 64520 | tf_op jit(solution)/shard_map/ppermute | solution.py:19
  259.7 5.9 %collective-permute-start.11 = (f32[7,1,768]{2,1,0:T(1,128)S(1)}, f32[7,1,768]{2,1,0:T(1,128)S(1)}, u32[]{:S(2)}, u32[]{:S(2)}) collective-permute-start(f32[7,1,768]{2,1,0:T(1,128)S(1)} %get-tuple-element.12), channel_id=1, source_target_pairs={{0,1},{1,2},{2,3},{3,4},{4,5},{5,6},{6,7},{7,8},{8,9},{9,10},{10,1... | collective-permute-start | bytes 64520 | tf_op jit(solution)/shard_map/ppermute | solution.py:17
  262.2 6.9 %collective-permute-start.10 = (f32[7,1,768]{2,1,0:T(1,128)S(1)}, f32[7,1,768]{2,1,0:T(1,128)S(1)}, u32[]{:S(2)}, u32[]{:S(2)}) collective-permute-start(f32[7,1,768]{2,1,0:T(1,128)S(1)} %get-tuple-element.13), channel_id=1, source_target_pairs={{1,0},{2,1},{3,2},{4,3},{5,4},{6,5},{7,6},{8,7},{9,8},{10,9},{11,1... | collective-permute-start | bytes 64520 | tf_op jit(solution)/shard_map/ppermute | solution.py:19
  270.1 5.9 %collective-permute-start.13 = (f32[7,1,768]{2,1,0:T(1,128)S(1)}, f32[7,1,768]{2,1,0:T(1,128)S(1)}, u32[]{:S(2)}, u32[]{:S(2)}) collective-permute-start(f32[7,1,768]{2,1,0:T(1,128)S(1)} %get-tuple-element.10), channel_id=1, source_target_pairs={{0,1},{1,2},{2,3},{3,4},{4,5},{5,6},{6,7},{7,8},{8,9},{9,10},{10,1... | collective-permute-start | bytes 64520 | tf_op jit(solution)/shard_map/ppermute | solution.py:17
  274.0 6.8 %collective-permute-start.12 = (f32[7,1,768]{2,1,0:T(1,128)S(1)}, f32[7,1,768]{2,1,0:T(1,128)S(1)}, u32[]{:S(2)}, u32[]{:S(2)}) collective-permute-start(f32[7,1,768]{2,1,0:T(1,128)S(1)} %get-tuple-element.11), channel_id=1, source_target_pairs={{1,0},{2,1},{3,2},{4,3},{5,4},{6,5},{7,6},{8,7},{9,8},{10,9},{11,1... | collective-permute-start | bytes 64520 | tf_op jit(solution)/shard_map/ppermute | solution.py:19
  281.8 5.9 %collective-permute-start.15 = (f32[7,1,768]{2,1,0:T(1,128)S(1)}, f32[7,1,768]{2,1,0:T(1,128)S(1)}, u32[]{:S(2)}, u32[]{:S(2)}) collective-permute-start(f32[7,1,768]{2,1,0:T(1,128)S(1)} %get-tuple-element.8), channel_id=1, source_target_pairs={{0,1},{1,2},{2,3},{3,4},{4,5},{5,6},{6,7},{7,8},{8,9},{9,10},{10,1... | collective-permute-start | bytes 64520 | tf_op jit(solution)/shard_map/ppermute | solution.py:17
  284.7 6.6 %collective-permute-start.14 = (f32[7,1,768]{2,1,0:T(1,128)S(1)}, f32[7,1,768]{2,1,0:T(1,128)S(1)}, u32[]{:S(2)}, u32[]{:S(2)}) collective-permute-start(f32[7,1,768]{2,1,0:T(1,128)S(1)} %get-tuple-element.9), channel_id=1, source_target_pairs={{1,0},{2,1},{3,2},{4,3},{5,4},{6,5},{7,6},{8,7},{9,8},{10,9},{11,1... | collective-permute-start | bytes 64520 | tf_op jit(solution)/shard_map/ppermute | solution.py:19
where the time goes:
time: 294 us
  blocking collectives  129 us (44%)
  local copies, waits for them, and re-layouts  51 us (17%)
  starting transfers between devices  47.5 us (16%)
  waiting for transfers between devices  34.9 us (12%)
  other arithmetic  30 us (10%)
    psum x1, blocking collectives, body(): summed = lax.psum(picked, 'mem')  129 us
    ppermute x8, waiting for transfers between devices, with_halo(): lax.ppermute(head, axis, [((i + 1) % count, i) for i in range(ends)])  34.9 us
    ppermute x8, starting transfers between devices, with_halo(): lax.ppermute(tail, axis, [(i, (i + 1) % count) for i in range(ends)])  28.9 us
    gather x1, local copies, waits for them, and re-layouts, body(): observed = summed + moved_static.reshape(-1)[cells_here]  23 us
    gather x1, local copies, waits for them, and re-layouts, body(): picked = partial_value.reshape(-1)[cells_here]  23 us
    scatter-add x1, other arithmetic, body(): forcing = jnp.zeros((moved_static.size,), jnp.float32).at[cells_here].add...  22 us
    ppermute x8, starting transfers between devices, with_halo(): lax.ppermute(head, axis, [((i + 1) % count, i) for i in range(ends)])  18.5 us
  transfers between devices with their start and end apart: 16, of which 8 were waited for; matrix products, arithmetic and copies ran while one was open for 0% of the time, Pallas kernels for 0%

commit v1 on v0

v1 whole, which is shorter than its diff:
```python
import functools

import jax
import jax.numpy as jnp
from jax import lax
from jax.experimental import pallas as pl
from jax.experimental.pallas import tpu as pltpu
from jax.sharding import PartitionSpec as P

MESH = pl.DeviceIdType.MESH
STEPS = 4
NVAR = 4
PAD = 8
LANES = 128
WIDE = 256


def beside_all(field):
    rows, cols = field.shape
    col = lax.broadcasted_iota(jnp.int32, field.shape, 1)
    above = pltpu.roll(field, 1, 0)
    below = pltpu.roll(field, rows - 1, 0)
    before = jnp.where(col == 0, 0.0, pltpu.roll(field, 1, 1))
    after = jnp.where(col == cols - 1, 0.0, pltpu.roll(field, cols - 1, 1))
    return above + below + before + after


def forward(field, kappa):
    for step in range(STEPS):
        field = field + kappa * (beside_all(field) - 4.0 * field)
    return field


def adjoint(field, kappa):
    for step in range(STEPS):
        weighted = kappa * field
        field = field + (beside_all(weighted) - 4.0 * weighted)
    return field


def kernel(
    tiles,
    members,
    alpha_hbm,
    static_hbm,
    pert_hbm,
    table_hbm,
    class_hbm,
    cells_hbm,
    counts_hbm,
    innov_hbm,
    weights_hbm,
    out_alpha,
    out_static,
    ext,
    kappa_ext,
    pert,
    classes,
    cells,
    innov,
    weights,
    table,
    counts,
    fwd_send,
    fwd_recv,
    static_send,
    static_recv,
    adj_send,
    adj_recv,
    inc,
    split,
    hot_lane,
    hot_row,
    obs,
    pair_buf,
    ring_buf,
    resid,
    adj,
    in_sem,
    fwd_sems,
    static_sems,
    adj_sems,
    pair_sems,
    ring_sems,
    swap_sems,
):
    owned, rows, cols = alpha_hbm.shape
    depth = members // 4
    slots = cells.shape[0]
    half = slots // 2
    scale = (owned * members - 1.0) ** (-0.5)
    m = lax.axis_index("mem")
    t = lax.axis_index("tile")
    core = lax.rem(m, 2)
    quad = lax.rem(m, 4)
    far = quad // 2
    level = m // 4
    stride = members // NVAR
    owner = lax.rem(m, stride) == 0
    var = m // stride
    has_up = t > 0
    has_down = t < tiles - 1

    core_mate = m + 1 - 2 * core
    far_mate = m + 2 - 4 * far
    both_mate = core_mate + 2 - 4 * far

    barrier = pltpu.get_barrier_semaphore()
    for mate in (core_mate, far_mate, both_mate):
        pl.semaphore_signal(barrier, inc=1, device_id={"mem": mate}, device_id_type=MESH)
    for d in range(1, depth):
        mate = lax.rem(level + d, depth) * 4 + quad
        pl.semaphore_signal(barrier, inc=1, device_id={"mem": mate}, device_id_type=MESH)

    @pl.when(has_up)
    def _():
        pl.semaphore_signal(barrier, inc=1, device_id={"tile": t - 1}, device_id_type=MESH)

    @pl.when(has_down)
    def _():
        pl.semaphore_signal(barrier, inc=1, device_id={"tile": t + 1}, device_id_type=MESH)

    own = pl.ds(PAD, rows)
    loads = [
        pltpu.make_async_copy(class_hbm, classes, in_sem.at[0]),
        pltpu.make_async_copy(table_hbm, table, in_sem.at[1]),
        pltpu.make_async_copy(alpha_hbm, ext.at[pl.ds(0, owned), own], in_sem.at[2]),
        pltpu.make_async_copy(static_hbm.at[var], ext.at[owned, own], in_sem.at[3]),
        pltpu.make_async_copy(cells_hbm, cells, in_sem.at[4]),
        pltpu.make_async_copy(counts_hbm, counts, in_sem.at[5]),
        pltpu.make_async_copy(innov_hbm, innov, in_sem.at[6]),
        pltpu.make_async_copy(weights_hbm, weights, in_sem.at[7]),
        pltpu.make_async_copy(pert_hbm, pert, in_sem.at[8]),
    ]
    for load in loads:
        load.start()

    for edge, missing in ((0, t == 0), (1, t == tiles - 1)):

        @pl.when(missing)
        def _():
            fwd_recv[edge] = jnp.zeros(fwd_recv.shape[1:], jnp.float32)
            static_recv[edge] = jnp.zeros(static_recv.shape[1:], jnp.float32)
            adj_recv[edge] = jnp.zeros(adj_recv.shape[1:], jnp.float32)

    def exchange(send, recv, sems):
        up = pltpu.make_async_remote_copy(
            send.at[0], recv.at[1], sems.at[0, 0], sems.at[1, 1], device_id={"tile": t - 1}, device_id_type=MESH
        )
        down = pltpu.make_async_remote_copy(
            send.at[1], recv.at[0], sems.at[0, 1], sems.at[1, 0], device_id={"tile": t + 1}, device_id_type=MESH
        )
        return up, down

    def start(pair):
        @pl.when(has_up)
        def _():
            pair[0].start()

        @pl.when(has_down)
        def _():
            pair[1].start()

    def wait(pair):
        @pl.when(has_up)
        def _():
            pair[0].wait_send()
            pair[1].wait_recv()

        @pl.when(has_down)
        def _():
            pair[1].wait_send()
            pair[0].wait_recv()

    loads[0].wait()
    loads[1].wait()
    kind = classes[...]
    kappa = jnp.full(kind.shape, table[0], jnp.float32)
    for i in range(1, table.shape[0]):
        kappa = jnp.where(kind == i, table[i], kappa)
    kappa_ext[own] = kappa
    fwd_send[0, pl.ds(4 * owned, STEPS)] = kappa[:STEPS]
    fwd_send[1, pl.ds(4 * owned, STEPS)] = kappa[rows - STEPS :]
    loads[2].wait()
    for f in range(owned):
        fwd_send[0, pl.ds(4 * f, STEPS)] = ext[f, pl.ds(PAD, STEPS)]
        fwd_send[1, pl.ds(4 * f, STEPS)] = ext[f, pl.ds(PAD + rows - STEPS, STEPS)]
    loads[3].wait()
    static_send[0] = ext[owned, pl.ds(PAD, STEPS)]
    static_send[1] = ext[owned, pl.ds(PAD + rows - STEPS, STEPS)]

    pl.semaphore_wait(barrier, depth + 2 + has_up.astype(jnp.int32) + has_down.astype(jnp.int32))
    fwd_pair = exchange(fwd_send, fwd_recv, fwd_sems)
    start(fwd_pair)
    static_pair = exchange(static_send, static_recv, static_sems)

    @pl.when(owner)
    def _():
        start(static_pair)

    loads[4].wait()
    folds = cols // WIDE
    field_rows = NVAR * rows
    lane_of = lax.broadcasted_iota(jnp.int32, (WIDE, LANES), 0)
    row_of = lax.broadcasted_iota(jnp.int32, (folds * field_rows, LANES), 0)
    row_of = lax.rem(row_of, field_rows) * folds + row_of // field_rows

    def make_hot(i, carry):
        at = pl.ds(pl.multiple_of(i * LANES, LANES), LANES)
        cell = cells[pl.ds(i, 1), :]
        hot_lane[:, at] = jnp.where(lane_of == lax.rem(cell, WIDE), 1.0, 0.0).astype(jnp.bfloat16)
        hot_row[:, at] = jnp.where(row_of == cell // WIDE, 1.0, 0.0).astype(jnp.bfloat16)
        return carry

    lax.fori_loop(0, slots, make_hot, 0)
    for load in loads[5:]:
        load.wait()

    wait(fwd_pair)

    def with_rows(ref, f, above, below):
        blank = jnp.zeros((PAD - STEPS, cols), jnp.float32)
        ref[f, pl.ds(0, PAD)] = jnp.concatenate([blank, above], 0)
        ref[f, pl.ds(PAD + rows, PAD)] = jnp.concatenate([below, blank], 0)

    blank = jnp.zeros((PAD - STEPS, cols), jnp.float32)
    kappa_ext[pl.ds(0, PAD)] = jnp.concatenate([blank, fwd_recv[0, pl.ds(4 * owned, STEPS)]], 0)
    kappa_ext[pl.ds(PAD + rows, PAD)] = jnp.concatenate([fwd_recv[1, pl.ds(4 * owned, STEPS)], blank], 0)
    for f in range(owned):
        with_rows(ext, f, fwd_recv[0, pl.ds(4 * f, STEPS)], fwd_recv[1, pl.ds(4 * f, STEPS)])

    inc[...] = jnp.zeros(inc.shape, jnp.float32)

    def move(f, carry):
        moved = forward(ext[f], kappa_ext[...])[PAD : PAD + rows] * scale
        for v in range(NVAR):
            inc[v] = inc[v] + pert[f, v].astype(jnp.float32) * moved
        return carry

    lax.fori_loop(0, owned, move, 0)

    @pl.when(owner)
    def _():
        wait(static_pair)
        with_rows(ext, owned, static_recv[0], static_recv[1])
        inc[var] = inc[var] + forward(ext[owned], kappa_ext[...])[PAD : PAD + rows]

    for fold in range(folds):
        part = inc[:, :, pl.ds(fold * WIDE, WIDE)].reshape(field_rows, WIDE)
        high = part.astype(jnp.bfloat16)
        low = (part - high.astype(jnp.float32)).astype(jnp.bfloat16)
        split[0, pl.ds(fold * field_rows, field_rows)] = high
        split[1, pl.ds(fold * field_rows, field_rows)] = low

    row_wide = lax.broadcasted_iota(jnp.int32, (folds * field_rows, WIDE), 0)
    row_wide = lax.rem(row_wide, field_rows) * folds + row_wide // field_rows

    def pick(i, carry):
        at = pl.ds(pl.multiple_of(i * WIDE, WIDE), WIDE)
        hot = hot_lane[:, at]
        found = jnp.dot(split[0], hot, preferred_element_type=jnp.float32)
        found = found + jnp.dot(split[1], hot, preferred_element_type=jnp.float32)
        cell = jnp.concatenate([cells[pl.ds(2 * i, 1), :], cells[pl.ds(2 * i + 1, 1), :]], 1)
        value = jnp.sum(jnp.where(row_wide == cell // WIDE, found, 0.0), 0, keepdims=True)
        obs[pl.ds(2 * i, 1), :] = value[:, :LANES]
        obs[pl.ds(2 * i + 1, 1), :] = value[:, LANES:]
        return carry

    mine = pl.ds(pl.multiple_of(core * half, 8), half)
    others = pl.ds(pl.multiple_of((1 - core) * half, 8), half)
    blocks = half // 2

    def pair_copy(source, mate, sender, at):
        return pltpu.make_async_remote_copy(
            source, pair_buf.at[sender], pair_sems.at[0, at], pair_sems.at[1, sender], device_id={"mem": mate}, device_id_type=MESH
        )

    lax.fori_loop((1 - core) * blocks, (2 - core) * blocks, pick, 0)
    pair_core = pair_copy(obs.at[others], core_mate, quad, 0)
    pair_both = pair_copy(obs.at[others], both_mate, quad, 1)
    pair_core.start()
    pair_both.start()
    lax.fori_loop(core * blocks, (core + 1) * blocks, pick, 0)
    pair_far = pair_copy(obs.at[mine], far_mate, quad, 2)
    pair_far.start()
    pair_buf[quad] = obs[mine]
    for mate in (core_mate, far_mate, both_mate):
        pair_copy(obs.at[mine], mate, lax.rem(mate, 4), 0).wait_recv()
    ring_buf[level] = pair_buf[0] + pair_buf[1] + pair_buf[2] + pair_buf[3]

    def ring_copy(d):
        to = lax.rem(level + d, depth) * 4 + quad
        return pltpu.make_async_remote_copy(
            ring_buf.at[level], ring_buf.at[level], ring_sems.at[0, d], ring_sems.at[1, level], device_id={"mem": to}, device_id_type=MESH
        )

    for d in range(1, depth):
        ring_copy(d).start()
    for d in range(1, depth):
        other = lax.rem(level + d, depth)
        pltpu.make_async_remote_copy(
            ring_buf.at[other],
            ring_buf.at[other],
            ring_sems.at[0, d],
            ring_sems.at[1, other],
            device_id={"mem": other * 4 + quad},
            device_id_type=MESH,
        ).wait_recv()
    observed = ring_buf[0]
    for d in range(1, depth):
        observed = observed + ring_buf[d]
    slot = lax.broadcasted_iota(jnp.int32, (half, LANES), 0) * LANES + lax.broadcasted_iota(jnp.int32, (half, LANES), 1)
    slot = slot + core * (half * LANES)
    resid[mine] = jnp.where(slot < counts[0], (observed - innov[mine]) * weights[mine], 0.0)
    swap = pltpu.make_async_remote_copy(
        resid.at[mine], resid.at[mine], swap_sems.at[0], swap_sems.at[1], device_id={"mem": core_mate}, device_id_type=MESH
    )
    swap.start()

    def spread(first):
        def add(i, total):
            at = pl.ds(pl.multiple_of((first + i) * WIDE, WIDE), WIDE)
            value = jnp.concatenate([resid[pl.ds(2 * (first + i), 1), :], resid[pl.ds(2 * (first + i) + 1, 1), :]], 1)
            high = value.astype(jnp.bfloat16)
            low = (value - high.astype(jnp.float32)).astype(jnp.bfloat16)
            hot = hot_lane[:, at]
            both = jnp.concatenate([hot * high, hot * low], 1)
            rows_hot = hot_row[:, at]
            return total + lax.dot_general(
                jnp.concatenate([rows_hot, rows_hot], 1), both, (((1,), (1,)), ((), ())), preferred_element_type=jnp.float32
            )

        return lax.fori_loop(0, blocks, add, jnp.zeros((folds * field_rows, WIDE), jnp.float32))

    first_part = spread(core * blocks)
    swap.wait()
    forcing = first_part + spread((1 - core) * blocks)
    for fold in range(folds):
        part = forcing[fold * field_rows : (fold + 1) * field_rows]
        adj[pl.ds(owned, NVAR), own, pl.ds(fold * WIDE, WIDE)] = part.reshape(NVAR, rows, WIDE)

    def weigh(f, carry):
        total = pert[f, 0].astype(jnp.float32) * adj[owned, own]
        for v in range(1, NVAR):
            total = total + pert[f, v].astype(jnp.float32) * adj[owned + v, own]
        adj[f, own] = scale * total
        return carry

    lax.fori_loop(0, owned, weigh, 0)
    for f in range(owned + NVAR):
        adj_send[0, pl.ds(4 * f, STEPS)] = adj[f, pl.ds(PAD, STEPS)]
        adj_send[1, pl.ds(4 * f, STEPS)] = adj[f, pl.ds(PAD + rows - STEPS, STEPS)]
    adj_pair = exchange(adj_send, adj_recv, adj_sems)
    start(adj_pair)
    pair_core.wait_send()
    pair_both.wait_send()
    pair_far.wait_send()
    for d in range(1, depth):
        ring_copy(d).wait_send()
    wait(adj_pair)
    for f in range(owned + NVAR):
        with_rows(adj, f, adj_recv[0, pl.ds(4 * f, STEPS)], adj_recv[1, pl.ds(4 * f, STEPS)])

    def finish_alpha(f, carry):
        out_alpha[f] = adjoint(adj[f], kappa_ext[...])[PAD : PAD + rows]
        return carry

    def finish_static(v, carry):
        out_static[v] = adjoint(adj[owned + v], kappa_ext[...])[PAD : PAD + rows]
        return carry

    lax.fori_loop(0, owned, finish_alpha, 0)
    lax.fori_loop(0, NVAR, finish_static, 0)


def body(tiles, members, alpha_fields, static_control, perturbations, coef_table, coef_class, obs_cells, obs_counts, innovations, obs_weights):
    owned, rows, cols = alpha_fields.shape
    slots = obs_cells.shape[1] // LANES
    folded = (slots, LANES)
    half = slots // 2
    depth = members // 4
    fields = owned + NVAR
    packed = 4 * (owned + 1)
    adj_packed = -(-4 * fields // 8) * 8
    deep = rows + 2 * PAD
    field_rows = cols // WIDE * NVAR * rows
    f32, bf16, i32 = jnp.float32, jnp.bfloat16, jnp.int32
    anywhere = pl.BlockSpec(memory_space=pl.ANY)
    in_vmem = pl.BlockSpec(memory_space=pltpu.VMEM)
    dma = pltpu.SemaphoreType.DMA
    moved = pl.pallas_call(
        functools.partial(kernel, tiles, members),
        out_shape=(jax.ShapeDtypeStruct((owned, rows, cols), f32), jax.ShapeDtypeStruct((NVAR, rows, cols), f32)),
        in_specs=[anywhere] * 9,
        out_specs=(in_vmem, in_vmem),
        scratch_shapes=[
            pltpu.VMEM((owned + 1, deep, cols), f32),
            pltpu.VMEM((deep, cols), f32),
            pltpu.VMEM((owned, NVAR, rows, cols), bf16),
            pltpu.VMEM((rows, cols), i32),
            pltpu.VMEM(folded, i32),
            pltpu.VMEM(folded, f32),
            pltpu.VMEM(folded, f32),
            pltpu.SMEM(coef_table.shape, f32),
            pltpu.SMEM(obs_counts.shape, i32),
            pltpu.VMEM((2, packed, cols), f32),
            pltpu.VMEM((2, packed, cols), f32),
            pltpu.VMEM((2, STEPS, cols), f32),
            pltpu.VMEM((2, STEPS, cols), f32),
            pltpu.VMEM((2, adj_packed, cols), f32),
            pltpu.VMEM((2, adj_packed, cols), f32),
            pltpu.VMEM((NVAR, rows, cols), f32),
            pltpu.VMEM((2, field_rows, WIDE), bf16),
            pltpu.VMEM((WIDE, slots * LANES), bf16),
            pltpu.VMEM((field_rows, slots * LANES), bf16),
            pltpu.VMEM(folded, f32),
            pltpu.VMEM((4, half, LANES), f32),
            pltpu.VMEM((depth, half, LANES), f32),
            pltpu.VMEM(folded, f32),
            pltpu.VMEM((fields, deep, cols), f32),
            dma((9,)),
            dma((2, 2)),
            dma((2, 2)),
            dma((2, 2)),
            dma((2, 4)),
            dma((2, depth)),
            dma((2,)),
        ],
        compiler_params=pltpu.CompilerParams(collective_id=0, has_side_effects=True),
    )(
        alpha_fields,
        static_control,
        perturbations,
        coef_table,
        coef_class,
        obs_cells.reshape(folded),
        obs_counts,
        innovations.reshape(folded),
        obs_weights.reshape(folded),
    )
    return alpha_fields + moved[0], static_control + moved[1]


def solution(mesh):
    in_specs = (
        P("mem", "tile", None),
        P(None, "tile", None),
        P("mem", None, "tile", None),
        P(),
        P("tile", None),
        P("tile", None),
        P("tile"),
        P("tile", None),
        P("tile", None),
    )
    out_specs = (P("mem", "tile", None), P(None, "tile", None))
    run = functools.partial(body, mesh.shape["tile"], mesh.shape["mem"])
    return jax.shard_map(run, mesh=mesh, in_specs=in_specs, out_specs=out_specs, check_vma=False)
```

time: 294 us -> 48.2 us (0.16)
  the two profiles are of different devices: /device:TPU:130 before, /device:TPU:4 now
where the time goes in v1:
time: 48.2 us; the launch traced here: 48.1 us
  Pallas kernels  44.2 us (92%)
  other arithmetic  2.57 us (5%)
  between operations  1.32 us (3%)
    pallas_call x1, Pallas kernels, body(): pl.pallas_call(functools.partial(kernel, tiles, members), out_shape=(jax....  44.2 us
    add x2, other arithmetic, body(): return (alpha_fields + moved[0], static_control + moved[1])  2.57 us

profile of v1, /device:TPU:4, one launch (start us, length us, event | category | flops | bytes accessed | tf_op | source)
XLA Modules:
  0.0 48.1 jit_solution(18221303934247055153)
XLA Ops:
  1.3 0.0 copy-start.1
  1.3 44.2 %shard_map.104 = (f32[3,32,768]{2,1,0:T(8,128)}, f32[4,32,768]{2,1,0:T(8,128)}) custom-call(f32[3,32,768]{2,1,0:T(8,128)} %alpha_hbm.1, f32[4,32,768]{2,1,0:T(8,128)} %static_hbm.1, bf16[3,4,32,768]{3,2,1,0:T(8,128)(2,1)} %pert_hbm.1, f32[8]{0:T(128)} %table_hbm.1, s32[32,768]{1,0:T(8,128)} %class_hbm.1, s32[32,128]{1,0:T(8,128)} %bitcast.3, ...), custom_call_target="tpu_custom_call" | custom-call | tf_op jit(solution)/shard_map/pallas_call | solution.py:391
  45.4 0.0 copy-done.1
  45.5 0.0 copy-start
  45.5 0.0 copy-start.2
  45.5 1.8 %add.6 = f32[3,32,768]{2,1,0:T(8,128)} add(f32[3,32,768]{2,1,0:T(8,128)S(1)} %copy-done.1, f32[3,32,768]{2,1,0:T(8,128)} %get-tuple-element.4) | non-fusion elementwise | flops 73728 | bytes 884736 | tf_op jit(solution)/shard_map/add | solution.py:441
  47.3 0.0 copy-done
  47.3 0.0 copy-done.2
  47.3 0.8 %add.7 = f32[4,32,768]{2,1,0:T(8,128)} add(f32[4,32,768]{2,1,0:T(8,128)S(1)} %copy-done, f32[4,32,768]{2,1,0:T(8,128)S(1)} %copy-done.2) | non-fusion elementwise | flops 98304 | bytes 1179648 | tf_op jit(solution)/shard_map/add | solution.py:441
Async XLA Ops:
  1.3 44.2 %copy-start.1 = (f32[3,32,768]{2,1,0:T(8,128)S(1)}, f32[3,32,768]{2,1,0:T(8,128)}, u32[]{:S(2)}) copy-start(f32[3,32,768]{2,1,0:T(8,128)} %alpha_hbm.1) | copy-start | bytes 884740
  45.5 1.8 %copy-start = (f32[4,32,768]{2,1,0:T(8,128)S(1)}, f32[4,32,768]{2,1,0:T(8,128)}, u32[]{:S(2)}) copy-start(f32[4,32,768]{2,1,0:T(8,128)} %static_hbm.1) | copy-start | bytes 1179652
  45.5 1.8 %copy-start.2 = (f32[4,32,768]{2,1,0:T(8,128)S(1)}, f32[4,32,768]{2,1,0:T(8,128)}, u32[]{:S(2)}) copy-start(f32[4,32,768]{2,1,0:T(8,128)} %get-tuple-element.5) | copy-start | bytes 1179652

commit v2 on v1

v2 whole, which is shorter than its diff:
```python
import functools

import jax
import jax.numpy as jnp
from jax import lax
from jax.experimental import pallas as pl
from jax.experimental.pallas import tpu as pltpu
from jax.sharding import PartitionSpec as P

MESH = pl.DeviceIdType.MESH
STEPS = 4
NVAR = 4
PAD = 8
LANES = 128
WIDE = 256
CHUNK = 1024


def advance(source, target, kappa, keep, f, starts):
    tiles = source.shape[1]
    lane = lax.broadcasted_iota(jnp.int32, (8, LANES), 1)
    first, last = lane == 0, lane == LANES - 1
    for r in starts:
        here = [source[f, j, pl.ds(r, 8), :] for j in range(tiles)]
        right = [pltpu.roll(a, 1, 1) for a in here]
        left = [pltpu.roll(a, LANES - 1, 1) for a in here]
        for j in range(tiles):
            before = jnp.where(first, right[j - 1] if j else 0.0, right[j])
            after = jnp.where(last, left[j + 1] if j < tiles - 1 else 0.0, left[j])
            around = (source[f, j, pl.ds(r - 1, 8), :] + source[f, j, pl.ds(r + 1, 8), :]) + (before + after)
            target[f, j, pl.ds(r, 8), :] = keep[j, pl.ds(r, 8), :] * here[j] + kappa[j, pl.ds(r, 8), :] * around


def inner_rows(stages, kappa, keep, f, rows):
    for s in range(STEPS):
        advance(stages[s], stages[s + 1], kappa, keep, f, range(PAD, PAD + rows, 8))


def border_rows(stages, kappa, keep, fields, rows):
    for s in range(STEPS):
        for f in fields:
            advance(stages[s], stages[s + 1], kappa, keep, f, (PAD - STEPS + s, PAD + rows - STEPS - s))


def kernel(
    tiles,
    members,
    alpha_hbm,
    static_hbm,
    pert_hbm,
    table_hbm,
    class_hbm,
    cells_hbm,
    counts_hbm,
    innov_hbm,
    weights_hbm,
    out_alpha,
    out_static,
    alpha,
    static,
    pert,
    classes,
    cells,
    innov,
    weights,
    table,
    counts,
    kappa,
    keep,
    inverse,
    fwd0,
    fwd1,
    fwd2,
    fwd3,
    fwd4,
    adj0,
    adj1,
    adj2,
    adj3,
    adj4,
    fwd_send,
    fwd_recv,
    static_send,
    static_recv,
    adj_send,
    adj_recv,
    field,
    split,
    hot_lane,
    hot_row,
    obs,
    pair_buf,
    ring_buf,
    resid,
    in_sem,
    fwd_sems,
    static_sems,
    adj_sems,
    pair_sems,
    ring_sems,
    swap_sems,
):
    owned, rows, cols = alpha.shape
    lane_tiles = cols // LANES
    folds = cols // WIDE
    field_rows = NVAR * rows
    depth = members // 4
    slots = cells.shape[0]
    half = slots // 2
    scale = (owned * members - 1.0) ** (-0.5)
    fwd = (fwd0, fwd1, fwd2, fwd3, fwd4)
    adj = (adj0, adj1, adj2, adj3, adj4)
    m = lax.axis_index("mem")
    t = lax.axis_index("tile")
    core = lax.rem(m, 2)
    quad = lax.rem(m, 4)
    far = quad // 2
    level = m // 4
    stride = members // NVAR
    owner = lax.rem(m, stride) == stride // 2
    var = m // stride
    has_up = t > 0
    has_down = t < tiles - 1

    core_mate = m + 1 - 2 * core
    far_mate = m + 2 - 4 * far
    both_mate = core_mate + 2 - 4 * far

    barrier = pltpu.get_barrier_semaphore()

    @pl.when(has_up)
    def _():
        pl.semaphore_signal(barrier, inc=1, device_id={"tile": t - 1}, device_id_type=MESH)

    @pl.when(has_down)
    def _():
        pl.semaphore_signal(barrier, inc=1, device_id={"tile": t + 1}, device_id_type=MESH)

    for mate in (core_mate, far_mate, both_mate):
        pl.semaphore_signal(barrier, inc=1, device_id={"mem": mate}, device_id_type=MESH)
    for d in range(1, depth):
        mate = lax.rem(level + d, depth) * 4 + quad
        pl.semaphore_signal(barrier, inc=1, device_id={"mem": mate}, device_id_type=MESH)

    loads = [
        pltpu.make_async_copy(class_hbm, classes, in_sem.at[0]),
        pltpu.make_async_copy(table_hbm, table, in_sem.at[1]),
        pltpu.make_async_copy(alpha_hbm, alpha, in_sem.at[2]),
        pltpu.make_async_copy(static_hbm, static, in_sem.at[3]),
        pltpu.make_async_copy(cells_hbm, cells, in_sem.at[4]),
        pltpu.make_async_copy(counts_hbm, counts, in_sem.at[5]),
        pltpu.make_async_copy(innov_hbm, innov, in_sem.at[6]),
        pltpu.make_async_copy(weights_hbm, weights, in_sem.at[7]),
        pltpu.make_async_copy(pert_hbm, pert, in_sem.at[8]),
    ]
    for load in loads:
        load.start()

    for edge, missing in ((0, t == 0), (1, t == tiles - 1)):

        @pl.when(missing)
        def _():
            fwd_recv[edge] = jnp.zeros(fwd_recv.shape[1:], jnp.float32)
            static_recv[edge] = jnp.zeros(static_recv.shape[1:], jnp.float32)
            adj_recv[edge] = jnp.zeros(adj_recv.shape[1:], jnp.float32)

    def exchange(send, recv, sems):
        up = pltpu.make_async_remote_copy(
            send.at[0], recv.at[1], sems.at[0, 0], sems.at[1, 1], device_id={"tile": t - 1}, device_id_type=MESH
        )
        down = pltpu.make_async_remote_copy(
            send.at[1], recv.at[0], sems.at[0, 1], sems.at[1, 0], device_id={"tile": t + 1}, device_id_type=MESH
        )
        return up, down

    def start(pair):
        @pl.when(has_up)
        def _():
            pair[0].start()

        @pl.when(has_down)
        def _():
            pair[1].start()

    def wait(pair):
        @pl.when(has_up)
        def _():
            pair[0].wait_send()
            pair[1].wait_recv()

        @pl.when(has_down)
        def _():
            pair[1].wait_send()
            pair[0].wait_recv()

    def pack(send, g, top, bottom):
        at = pl.ds(4 * (g % 2), STEPS)
        send[0, g // 2, at, :] = top
        send[1, g // 2, at, :] = bottom

    def unpack(recv, g, target, index):
        at = pl.ds(4 * (g % 2), STEPS)
        target[(*index, pl.ds(PAD - STEPS, STEPS), slice(None))] = recv[0, g // 2, at, :]
        target[(*index, pl.ds(PAD + rows, STEPS), slice(None))] = recv[1, g // 2, at, :]

    own = pl.ds(PAD, rows)
    top_rows = pl.ds(PAD, STEPS)
    bottom_rows = pl.ds(PAD + rows - STEPS, STEPS)
    columns = [pl.ds(j * LANES, LANES) for j in range(lane_tiles)]

    loads[0].wait()
    loads[1].wait()
    for j in range(lane_tiles):
        kind = classes[:, columns[j]]
        value = jnp.full(kind.shape, table[0], jnp.float32)
        for i in range(1, table.shape[0]):
            value = jnp.where(kind == i, table[i], value)
        kappa[j, own, :] = value
        keep[j, own, :] = 1.0 - 4.0 * value
        pack(fwd_send, owned * lane_tiles + j, value[:STEPS], value[rows - STEPS :])
    loads[2].wait()
    for f in range(owned):
        for j in range(lane_tiles):
            fwd0[f, j, own, :] = alpha[f, :, columns[j]]
            pack(fwd_send, f * lane_tiles + j, fwd0[f, j, top_rows, :], fwd0[f, j, bottom_rows, :])
    loads[3].wait()

    @pl.when(owner)
    def _():
        for j in range(lane_tiles):
            fwd0[owned, j, own, :] = static[var, :, columns[j]]
            pack(static_send, j, fwd0[owned, j, top_rows, :], fwd0[owned, j, bottom_rows, :])

    pl.semaphore_wait(barrier, depth + 2 + has_up.astype(jnp.int32) + has_down.astype(jnp.int32))
    fwd_pair = exchange(fwd_send, fwd_recv, fwd_sems)
    start(fwd_pair)
    static_pair = exchange(static_send, static_recv, static_sems)

    @pl.when(owner)
    def _():
        start(static_pair)

    loads[4].wait()
    lane_of = lax.broadcasted_iota(jnp.int32, (WIDE, LANES), 0)
    three_rows = folds * lax.broadcasted_iota(jnp.int32, (field_rows, LANES), 0)

    def make_hot_lane(i, carry):
        at = pl.ds(pl.multiple_of(i * LANES, LANES), LANES)
        hot_lane[:, at] = jnp.where(lane_of == (cells[pl.ds(i, 1), :] & (WIDE - 1)), 1.0, 0.0).astype(jnp.bfloat16)
        return carry

    def make_hot_row(i, carry):
        at = pl.ds(pl.multiple_of(i * LANES, LANES), LANES)
        row = cells[pl.ds(i, 1), :] // WIDE
        for fold in range(folds):
            hot = jnp.where(three_rows == row - fold, 1.0, 0.0).astype(jnp.bfloat16)
            hot_row[pl.ds(fold * field_rows, field_rows), at] = hot
        return carry

    lax.fori_loop(0, slots, make_hot_lane, 0)

    def inner_fwd(f, carry):
        inner_rows(fwd, kappa, keep, f, rows)
        return carry

    lax.fori_loop(0, owned, inner_fwd, 0)

    @pl.when(owner)
    def _():
        inner_rows(fwd, kappa, keep, owned, rows)

    for load in loads[5:]:
        load.wait()

    wait(fwd_pair)
    for j in range(lane_tiles):
        unpack(fwd_recv, owned * lane_tiles + j, kappa, (j,))
        for at in (pl.ds(PAD - STEPS, STEPS), pl.ds(PAD + rows, STEPS)):
            keep[j, at, :] = 1.0 - 4.0 * kappa[j, at, :]
        for f in range(owned):
            unpack(fwd_recv, f * lane_tiles + j, fwd0, (f, j))
    border_rows(fwd, kappa, keep, range(owned), rows)

    def place(v, j):
        return pl.ds((j * LANES // WIDE) * field_rows + v * rows, rows), pl.ds(j * LANES % WIDE, LANES)

    for j in range(lane_tiles):
        for v in range(NVAR):
            total = pert[0, v, :, columns[j]].astype(jnp.float32) * fwd4[0, j, own, :]
            for f in range(1, owned):
                total = total + pert[f, v, :, columns[j]].astype(jnp.float32) * fwd4[f, j, own, :]
            field[place(v, j)] = scale * total

    @pl.when(owner)
    def _():
        wait(static_pair)
        for j in range(lane_tiles):
            unpack(static_recv, j, fwd0, (owned, j))
        border_rows(fwd, kappa, keep, (owned,), rows)
        for j in range(lane_tiles):
            at = place(0, j)
            at = (pl.ds(pl.multiple_of(at[0].start + var * rows, rows), rows), at[1])
            field[at] = field[at] + fwd4[owned, j, own, :]

    high = field[...].astype(jnp.bfloat16)
    split[0] = high
    split[1] = (field[...] - high.astype(jnp.float32)).astype(jnp.bfloat16)

    per_chunk = CHUNK // LANES
    row_chunk = folds * lax.broadcasted_iota(jnp.int32, (field_rows, CHUNK), 0)

    def pick(i, carry):
        at = pl.ds(pl.multiple_of(i * CHUNK, CHUNK), CHUNK)
        hot = hot_lane[:, at]
        found = jnp.dot(split[0], hot, preferred_element_type=jnp.float32)
        found = found + jnp.dot(split[1], hot, preferred_element_type=jnp.float32)
        row = jnp.concatenate([cells[pl.ds(per_chunk * i + q, 1), :] for q in range(per_chunk)], 1) // WIDE
        kept = jnp.zeros((field_rows, CHUNK), jnp.float32)
        for fold in range(folds):
            kept = jnp.where(row_chunk == row - fold, found[fold * field_rows : (fold + 1) * field_rows], kept)
        value = jnp.sum(kept, 0, keepdims=True)
        for q in range(per_chunk):
            obs[pl.ds(per_chunk * i + q, 1), :] = value[:, q * LANES : (q + 1) * LANES]
        return carry

    mine = pl.ds(pl.multiple_of(core * half, 8), half)
    others = pl.ds(pl.multiple_of((1 - core) * half, 8), half)
    blocks = half // per_chunk

    def pair_copy(source, mate, sender, at):
        return pltpu.make_async_remote_copy(
            source, pair_buf.at[sender], pair_sems.at[0, at], pair_sems.at[1, sender], device_id={"mem": mate}, device_id_type=MESH
        )

    lax.fori_loop((1 - core) * blocks, (2 - core) * blocks, pick, 0)
    pair_both = pair_copy(obs.at[others], both_mate, quad, 1)
    pair_core = pair_copy(obs.at[others], core_mate, quad, 0)
    pair_both.start()
    pair_core.start()
    lax.fori_loop(core * blocks, (core + 1) * blocks, pick, 0)
    pair_far = pair_copy(obs.at[mine], far_mate, quad, 2)
    pair_far.start()
    pair_buf[quad] = obs[mine]
    lax.fori_loop(0, slots, make_hot_row, 0)
    for mate in (core_mate, far_mate, both_mate):
        pair_copy(obs.at[mine], mate, lax.rem(mate, 4), 0).wait_recv()
    ring_buf[level] = pair_buf[0] + pair_buf[1] + pair_buf[2] + pair_buf[3]

    def ring_copy(d):
        to = lax.rem(level + d, depth) * 4 + quad
        return pltpu.make_async_remote_copy(
            ring_buf.at[level], ring_buf.at[level], ring_sems.at[0, d], ring_sems.at[1, level], device_id={"mem": to}, device_id_type=MESH
        )

    order = sorted(range(1, depth), key=lambda d: -min(d, depth - d))
    for d in order:
        ring_copy(d).start()
    for j in range(lane_tiles):
        inverse[j] = 1.0 / kappa[j, own, :]
    for d in range(1, depth):
        other = lax.rem(level + d, depth)
        pltpu.make_async_remote_copy(
            ring_buf.at[other],
            ring_buf.at[other],
            ring_sems.at[0, d],
            ring_sems.at[1, other],
            device_id={"mem": other * 4 + quad},
            device_id_type=MESH,
        ).wait_recv()
    observed = ring_buf[0]
    for d in range(1, depth):
        observed = observed + ring_buf[d]
    slot = lax.broadcasted_iota(jnp.int32, (half, LANES), 0) * LANES + lax.broadcasted_iota(jnp.int32, (half, LANES), 1)
    slot = slot + core * (half * LANES)
    resid[mine] = jnp.where(slot < counts[0], (observed - innov[mine]) * weights[mine], 0.0)
    swap = pltpu.make_async_remote_copy(
        resid.at[mine], resid.at[mine], swap_sems.at[0], swap_sems.at[1], device_id={"mem": core_mate}, device_id_type=MESH
    )
    swap.start()

    def spread(which):
        at = pl.ds(pl.multiple_of(which * (half * LANES), half * LANES), half * LANES)
        value = jnp.concatenate([resid[pl.ds(which * half + q, 1), :] for q in range(half)], 1)
        high = value.astype(jnp.bfloat16)
        low = (value - high.astype(jnp.float32)).astype(jnp.bfloat16)
        hot = hot_lane[:, at]
        row = hot_row[:, at]
        return lax.dot_general(
            jnp.concatenate([row, row], 1),
            jnp.concatenate([hot * high, hot * low], 1),
            (((1,), (1,)), ((), ())),
            preferred_element_type=jnp.float32,
        )

    field[...] = spread(core)
    swap.wait()
    field[...] = field[...] + spread(1 - core)

    for j in range(lane_tiles):
        forcing = [field[place(v, j)] for v in range(NVAR)]
        factor = kappa[j, own, :]
        for v in range(NVAR):
            adj0[owned + v, j, own, :] = factor * forcing[v]
        for f in range(owned):
            total = pert[f, 0, :, columns[j]].astype(jnp.float32) * forcing[0]
            for v in range(1, NVAR):
                total = total + pert[f, v, :, columns[j]].astype(jnp.float32) * forcing[v]
            adj0[f, j, own, :] = factor * (scale * total)
        for f in range(owned + NVAR):
            pack(adj_send, f * lane_tiles + j, adj0[f, j, top_rows, :], adj0[f, j, bottom_rows, :])
    adj_pair = exchange(adj_send, adj_recv, adj_sems)
    start(adj_pair)

    def inner_adj(f, carry):
        inner_rows(adj, kappa, keep, f, rows)
        return carry

    lax.fori_loop(0, owned + NVAR, inner_adj, 0)
    pair_core.wait_send()
    pair_both.wait_send()
    pair_far.wait_send()
    for d in range(1, depth):
        ring_copy(d).wait_send()
    wait(adj_pair)
    for j in range(lane_tiles):
        for f in range(owned + NVAR):
            unpack(adj_recv, f * lane_tiles + j, adj0, (f, j))
    border_rows(adj, kappa, keep, range(owned + NVAR), rows)
    for j in range(lane_tiles):
        for f in range(owned):
            out_alpha[f, :, columns[j]] = alpha[f, :, columns[j]] + adj4[f, j, own, :] * inverse[j]
        for v in range(NVAR):
            out_static[v, :, columns[j]] = static[v, :, columns[j]] + adj4[owned + v, j, own, :] * inverse[j]


def body(tiles, members, alpha_fields, static_control, perturbations, coef_table, coef_class, obs_cells, obs_counts, innovations, obs_weights):
    owned, rows, cols = alpha_fields.shape
    slots = obs_cells.shape[1] // LANES
    folded = (slots, LANES)
    half = slots // 2
    depth = members // 4
    fields = owned + NVAR
    lane_tiles = cols // LANES
    deep = rows + 2 * PAD
    field_rows = cols // WIDE * NVAR * rows
    f32, bf16, i32 = jnp.float32, jnp.bfloat16, jnp.int32
    anywhere = pl.BlockSpec(memory_space=pl.ANY)
    in_hbm = functools.partial(pltpu.with_memory_space_constraint, memory_space=pltpu.HBM)
    in_vmem = pl.BlockSpec(memory_space=pltpu.VMEM)
    dma = pltpu.SemaphoreType.DMA

    def message(count):
        return [pltpu.VMEM((2, count * lane_tiles // 2, 8, LANES), f32)] * 2

    return pl.pallas_call(
        functools.partial(kernel, tiles, members),
        out_shape=(jax.ShapeDtypeStruct((owned, rows, cols), f32), jax.ShapeDtypeStruct((NVAR, rows, cols), f32)),
        in_specs=[anywhere] * 9,
        out_specs=(in_vmem, in_vmem),
        scratch_shapes=[
            pltpu.VMEM((owned, rows, cols), f32),
            pltpu.VMEM((NVAR, rows, cols), f32),
            pltpu.VMEM((owned, NVAR, rows, cols), bf16),
            pltpu.VMEM((rows, cols), i32),
            pltpu.VMEM(folded, i32),
            pltpu.VMEM(folded, f32),
            pltpu.VMEM(folded, f32),
            pltpu.SMEM(coef_table.shape, f32),
            pltpu.SMEM(obs_counts.shape, i32),
            pltpu.VMEM((lane_tiles, deep, LANES), f32),
            pltpu.VMEM((lane_tiles, deep, LANES), f32),
            pltpu.VMEM((lane_tiles, rows, LANES), f32),
            *[pltpu.VMEM((owned + 1, lane_tiles, deep, LANES), f32)] * (STEPS + 1),
            *[pltpu.VMEM((fields, lane_tiles, deep, LANES), f32)] * (STEPS + 1),
            *message(owned + 1),
            *message(1),
            *message(fields),
            pltpu.VMEM((field_rows, WIDE), f32),
            pltpu.VMEM((2, field_rows, WIDE), bf16),
            pltpu.VMEM((WIDE, slots * LANES), bf16),
            pltpu.VMEM((field_rows, slots * LANES), bf16),
            pltpu.VMEM(folded, f32),
            pltpu.VMEM((4, half, LANES), f32),
            pltpu.VMEM((depth, half, LANES), f32),
            pltpu.VMEM(folded, f32),
            dma((9,)),
            dma((2, 2)),
            dma((2, 2)),
            dma((2, 2)),
            dma((2, 4)),
            dma((2, depth)),
            dma((2,)),
        ],
        compiler_params=pltpu.CompilerParams(collective_id=0, has_side_effects=True, vmem_limit_bytes=48 * 2**20),
    )(
        in_hbm(alpha_fields),
        in_hbm(static_control),
        in_hbm(perturbations),
        in_hbm(coef_table),
        in_hbm(coef_class),
        in_hbm(obs_cells.reshape(folded)),
        obs_counts,
        in_hbm(innovations.reshape(folded)),
        in_hbm(obs_weights.reshape(folded)),
    )


def solution(mesh):
    in_specs = (
        P("mem", "tile", None),
        P(None, "tile", None),
        P("mem", None, "tile", None),
        P(),
        P("tile", None),
        P("tile", None),
        P("tile"),
        P("tile", None),
        P("tile", None),
    )
    out_specs = (P("mem", "tile", None), P(None, "tile", None))
    run = functools.partial(body, mesh.shape["tile"], mesh.shape["mem"])
    return jax.shard_map(run, mesh=mesh, in_specs=in_specs, out_specs=out_specs, check_vma=False)
```

time: 48.2 us -> 37.7 us (0.78)
  Pallas kernels: 44.2 us -> 34.8 us
  other arithmetic: 2.57 us -> 0 us
  local copies, waits for them, and re-layouts: 0.01 us -> 1.46 us
    pallas_call x1, Pallas kernels: 44.2 us -> 34.8 us  [body(): pl.pallas_call(functools.partial(kernel, tiles, members), out_shape=(jax....]
    add x2 -> x0, other arithmetic: 2.57 us -> none  [body(): return (alpha_fields + moved[0], static_control + moved[1])]
    unnamed x6 -> x2, local copies, waits for them, and re-layouts: 0.01 us -> 1.46 us
where the time goes in v2:
time: 37.7 us; the launch traced here: 37.6 us
  Pallas kernels  34.8 us (92%)
  local copies, waits for them, and re-layouts  1.46 us (4%)
  between operations  1.29 us (3%)
    pallas_call x1, Pallas kernels, body(): pl.pallas_call(functools.partial(kernel, tiles, members), out_shape=(jax....  34.8 us
    unnamed x2, local copies, waits for them, and re-layouts  1.46 us

profile of v2, /device:TPU:4, one launch (start us, length us, event | category | flops | bytes accessed | tf_op | source)
XLA Modules:
  0.0 37.6 jit_solution(9958665701532956219)
XLA Ops:
  1.3 34.8 %shard_map.104 = (f32[3,32,768]{2,1,0:T(8,128)S(1)}, f32[4,32,768]{2,1,0:T(8,128)S(1)}) custom-call(f32[3,32,768]{2,1,0:T(8,128)} %alpha_hbm.1, f32[4,32,768]{2,1,0:T(8,128)} %static_hbm.1, bf16[3,4,32,768]{3,2,1,0:T(8,128)(2,1)} %pert_hbm.1, f32[8]{0:T(128)} %table_hbm.1, s32[32,768]{1,0:T(8,128)} %class_hbm.1, s32[32,128]{1,0:T(8,128)} %bitcast.3, ...), custom_call_target="tpu_custom_call" | custom-call | tf_op jit(solution)/shard_map/pallas_call | solution.py:455
  36.1 0.7 %copy.14 = f32[3,32,768]{2,1,0:T(8,128)} copy(f32[3,32,768]{2,1,0:T(8,128)S(1)} %get-tuple-element.4) | data formatting | bytes 589824
  36.8 0.7 %copy.15 = f32[4,32,768]{2,1,0:T(8,128)} copy(f32[4,32,768]{2,1,0:T(8,128)S(1)} %get-tuple-element.5) | data formatting | bytes 786432

commit v3 on v2

--- a/solution.py
+++ b/solution.py
@@ -82,6 +82,8 @@
     fwd_recv,
     static_send,
     static_recv,
+    wide_send,
+    wide_recv,
     adj_send,
     adj_recv,
     field,
@@ -95,6 +97,7 @@
     in_sem,
     fwd_sems,
     static_sems,
+    wide_sems,
     adj_sems,
     pair_sems,
     ring_sems,
@@ -162,6 +165,7 @@
         def _():
             fwd_recv[edge] = jnp.zeros(fwd_recv.shape[1:], jnp.float32)
             static_recv[edge] = jnp.zeros(static_recv.shape[1:], jnp.float32)
+            wide_recv[edge] = jnp.zeros(wide_recv.shape[1:], jnp.float32)
             adj_recv[edge] = jnp.zeros(adj_recv.shape[1:], jnp.float32)
 
     def exchange(send, recv, sems):
@@ -341,7 +345,6 @@
     pair_far = pair_copy(obs.at[mine], far_mate, quad, 2)
     pair_far.start()
     pair_buf[quad] = obs[mine]
-    lax.fori_loop(0, slots, make_hot_row, 0)
     for mate in (core_mate, far_mate, both_mate):
         pair_copy(obs.at[mine], mate, lax.rem(mate, 4), 0).wait_recv()
     ring_buf[level] = pair_buf[0] + pair_buf[1] + pair_buf[2] + pair_buf[3]
@@ -355,6 +358,7 @@
     order = sorted(range(1, depth), key=lambda d: -min(d, depth - d))
     for d in order:
         ring_copy(d).start()
+    lax.fori_loop(0, slots, make_hot_row, 0)
     for j in range(lane_tiles):
         inverse[j] = 1.0 / kappa[j, own, :]
     for d in range(1, depth):
@@ -397,16 +401,17 @@
     field[...] = field[...] + spread(1 - core)
 
     for j in range(lane_tiles):
-        forcing = [field[place(v, j)] for v in range(NVAR)]
-        factor = kappa[j, own, :]
         for v in range(NVAR):
-            adj0[owned + v, j, own, :] = factor * forcing[v]
+            adj0[owned + v, j, own, :] = kappa[j, own, :] * field[place(v, j)]
+            pack(wide_send, v * lane_tiles + j, adj0[owned + v, j, top_rows, :], adj0[owned + v, j, bottom_rows, :])
+    wide_pair = exchange(wide_send, wide_recv, wide_sems)
+    start(wide_pair)
+    for j in range(lane_tiles):
         for f in range(owned):
-            total = pert[f, 0, :, columns[j]].astype(jnp.float32) * forcing[0]
+            total = pert[f, 0, :, columns[j]].astype(jnp.float32) * field[place(0, j)]
             for v in range(1, NVAR):
-                total = total + pert[f, v, :, columns[j]].astype(jnp.float32) * forcing[v]
-            adj0[f, j, own, :] = factor * (scale * total)
-        for f in range(owned + NVAR):
+                total = total + pert[f, v, :, columns[j]].astype(jnp.float32) * field[place(v, j)]
+            adj0[f, j, own, :] = kappa[j, own, :] * (scale * total)
             pack(adj_send, f * lane_tiles + j, adj0[f, j, top_rows, :], adj0[f, j, bottom_rows, :])
     adj_pair = exchange(adj_send, adj_recv, adj_sems)
     start(adj_pair)
@@ -421,16 +426,30 @@
     pair_far.wait_send()
     for d in range(1, depth):
         ring_copy(d).wait_send()
+    wait(wide_pair)
+    for j in range(lane_tiles):
+        for v in range(NVAR):
+            unpack(wide_recv, v * lane_tiles + j, adj0, (owned + v, j))
+    border_rows(adj, kappa, keep, range(owned, owned + NVAR), rows)
+    for j in range(lane_tiles):
+        for v in range(NVAR):
+            out_static[v, :, columns[j]] = static[v, :, columns[j]] + adj4[owned + v, j, own, :] * inverse[j]
     wait(adj_pair)
     for j in range(lane_tiles):
-        for f in range(owned + NVAR):
+        for f in range(owned):
             unpack(adj_recv, f * lane_tiles + j, adj0, (f, j))
-    border_rows(adj, kappa, keep, range(owned + NVAR), rows)
+    border_rows(adj, kappa, keep, range(owned), rows)
     for j in range(lane_tiles):
         for f in range(owned):
             out_alpha[f, :, columns[j]] = alpha[f, :, columns[j]] + adj4[f, j, own, :] * inverse[j]
-        for v in range(NVAR):
-            out_static[v, :, columns[j]] = static[v, :, columns[j]] + adj4[owned + v, j, own, :] * inverse[j]
+
+
+def write_out(alpha, static, out_alpha, out_static, sems):
+    copies = [pltpu.make_async_copy(alpha, out_alpha, sems.at[0]), pltpu.make_async_copy(static, out_static, sems.at[1])]
+    for copy in copies:
+        copy.start()
+    for copy in copies:
+        copy.wait()
 
 
 def body(tiles, members, alpha_fields, static_control, perturbations, coef_table, coef_class, obs_cells, obs_counts, innovations, obs_weights):
@@ -452,9 +471,10 @@
     def message(count):
         return [pltpu.VMEM((2, count * lane_tiles // 2, 8, LANES), f32)] * 2
 
-    return pl.pallas_call(
+    shapes = (jax.ShapeDtypeStruct((owned, rows, cols), f32), jax.ShapeDtypeStruct((NVAR, rows, cols), f32))
+    grads = pl.pallas_call(
         functools.partial(kernel, tiles, members),
-        out_shape=(jax.ShapeDtypeStruct((owned, rows, cols), f32), jax.ShapeDtypeStruct((NVAR, rows, cols), f32)),
+        out_shape=shapes,
         in_specs=[anywhere] * 9,
         out_specs=(in_vmem, in_vmem),
         scratch_shapes=[
@@ -474,7 +494,8 @@
             *[pltpu.VMEM((fields, lane_tiles, deep, LANES), f32)] * (STEPS + 1),
             *message(owned + 1),
             *message(1),
-            *message(fields),
+            *message(NVAR),
+            *message(owned),
             pltpu.VMEM((field_rows, WIDE), f32),
             pltpu.VMEM((2, field_rows, WIDE), bf16),
             pltpu.VMEM((WIDE, slots * LANES), bf16),
@@ -484,6 +505,7 @@
             pltpu.VMEM((depth, half, LANES), f32),
             pltpu.VMEM(folded, f32),
             dma((9,)),
+            dma((2, 2)),
             dma((2, 2)),
             dma((2, 2)),
             dma((2, 2)),
@@ -503,6 +525,14 @@
         in_hbm(innovations.reshape(folded)),
         in_hbm(obs_weights.reshape(folded)),
     )
+    return pl.pallas_call(
+        write_out,
+        out_shape=shapes,
+        in_specs=[anywhere, anywhere],
+        out_specs=(anywhere, anywhere),
+        scratch_shapes=[dma((2,))],
+        compiler_params=pltpu.CompilerParams(vmem_limit_bytes=2**20),
+    )(*grads)
 
 
 def solution(mesh):

time: 37.7 us -> 36.9 us (0.979)
  local copies, waits for them, and re-layouts: 1.46 us -> 0 us
  Pallas kernels: 34.8 us -> 35.4 us
    unnamed x2 -> x0, local copies, waits for them, and re-layouts: 1.46 us -> none
    pallas_call x1 -> x2, Pallas kernels: 34.8 us -> 35.4 us  [the longest x1 34.5 us: body(): pl.pallas_call(functools.partial(kernel, tiles, members), out_shape=shape...]
where the time goes in v3:
time: 36.9 us; the launch traced here: 36.7 us
  Pallas kernels  35.4 us (96%)
  between operations  1.29 us (3%)
    pallas_call x1, Pallas kernels, body(): pl.pallas_call(functools.partial(kernel, tiles, members), out_shape=shape...  34.5 us
    pallas_call x1, Pallas kernels, body(): pl.pallas_call(write_out, out_shape=shapes, in_specs=[anywhere, anywhere]...  0.86 us

profile of v3, /device:TPU:4, one launch (start us, length us, event | category | flops | bytes accessed | tf_op | source)
XLA Modules:
  0.0 36.7 jit_solution(6247664476039709811)
XLA Ops:
  1.3 34.5 %shard_map.104 = (f32[3,32,768]{2,1,0:T(8,128)S(1)}, f32[4,32,768]{2,1,0:T(8,128)S(1)}) custom-call(f32[3,32,768]{2,1,0:T(8,128)} %alpha_hbm.1, f32[4,32,768]{2,1,0:T(8,128)} %static_hbm.1, bf16[3,4,32,768]{3,2,1,0:T(8,128)(2,1)} %pert_hbm.1, f32[8]{0:T(128)} %table_hbm.1, s32[32,768]{1,0:T(8,128)} %class_hbm.1, s32[32,128]{1,0:T(8,128)} %bitcast.3, ...), custom_call_target="tpu_custom_call" | custom-call | tf_op jit(solution)/shard_map/pallas_call | solution.py:475
  35.8 0.9 %shard_map.105 = (f32[3,32,768]{2,1,0:T(8,128)}, f32[4,32,768]{2,1,0:T(8,128)}) custom-call(f32[3,32,768]{2,1,0:T(8,128)S(1)} %get-tuple-element.4.alpha, f32[4,32,768]{2,1,0:T(8,128)S(1)} %get-tuple-element.5.static), custom_call_target="tpu_custom_call" | custom-call | tf_op jit(solution)/shard_map/pallas_call | solution.py:528

commit v4 on v3

--- a/solution.py
+++ b/solution.py
@@ -37,9 +37,30 @@
 
 
 def border_rows(stages, kappa, keep, fields, rows):
+    tiles = kappa.shape[0]
+    lane = lax.broadcasted_iota(jnp.int32, (8, LANES), 1)
+    first, last = lane == 0, lane == LANES - 1
+    upper = lax.broadcasted_iota(jnp.int32, (8, LANES), 0) < 4
     for s in range(STEPS):
+        top, bottom = PAD - 3 + s, PAD + rows - 1 - s
+
+        def both(ref, index, shift):
+            return jnp.where(upper, ref[(*index, pl.ds(top + shift, 8))], ref[(*index, pl.ds(bottom - 4 + shift, 8))])
+
+        factor = [both(kappa, (j,), 0) for j in range(tiles)]
+        kept = [both(keep, (j,), 0) for j in range(tiles)]
+        source, target = stages[s], stages[s + 1]
         for f in fields:
-            advance(stages[s], stages[s + 1], kappa, keep, f, (PAD - STEPS + s, PAD + rows - STEPS - s))
+            here = [both(source, (f, j), 0) for j in range(tiles)]
+            right = [pltpu.roll(a, 1, 1) for a in here]
+            left = [pltpu.roll(a, LANES - 1, 1) for a in here]
+            for j in range(tiles):
+                before = jnp.where(first, right[j - 1] if j else 0.0, right[j])
+                after = jnp.where(last, left[j + 1] if j < tiles - 1 else 0.0, left[j])
+                around = (both(source, (f, j), -1) + both(source, (f, j), 1)) + (before + after)
+                value = kept[j] * here[j] + factor[j] * around
+                target[f, j, pl.ds(top, 4), :] = value[:4]
+                target[f, j, pl.ds(bottom, 4), :] = value[4:]
 
 
 def kernel(

time: 36.9 us -> 36.7 us (level)
  no operation moved by 1% of the time
where the time goes in v4:
time: 36.7 us; the launch traced here: 36.5 us
  Pallas kernels  35.3 us (96%)
  between operations  1.29 us (4%)
    pallas_call x1, Pallas kernels, body(): pl.pallas_call(functools.partial(kernel, tiles, members), out_shape=shape...  34.4 us
    pallas_call x1, Pallas kernels, body(): pl.pallas_call(write_out, out_shape=shapes, in_specs=[anywhere, anywhere]...  0.86 us

profile of v4, /device:TPU:4, one launch (start us, length us, event | category | flops | bytes accessed | tf_op | source)
XLA Modules:
  0.0 36.5 jit_solution(17573287993183644481)
XLA Ops:
  1.3 34.4 %shard_map.104 = (f32[3,32,768]{2,1,0:T(8,128)S(1)}, f32[4,32,768]{2,1,0:T(8,128)S(1)}) custom-call(f32[3,32,768]{2,1,0:T(8,128)} %alpha_hbm.1, f32[4,32,768]{2,1,0:T(8,128)} %static_hbm.1, bf16[3,4,32,768]{3,2,1,0:T(8,128)(2,1)} %pert_hbm.1, f32[8]{0:T(128)} %table_hbm.1, s32[32,768]{1,0:T(8,128)} %class_hbm.1, s32[32,128]{1,0:T(8,128)} %bitcast.3, ...), custom_call_target="tpu_custom_call" | custom-call | tf_op jit(solution)/shard_map/pallas_call | solution.py:496
  35.7 0.9 %shard_map.105 = (f32[3,32,768]{2,1,0:T(8,128)}, f32[4,32,768]{2,1,0:T(8,128)}) custom-call(f32[3,32,768]{2,1,0:T(8,128)S(1)} %get-tuple-element.4.alpha, f32[4,32,768]{2,1,0:T(8,128)S(1)} %get-tuple-element.5.static), custom_call_target="tpu_custom_call" | custom-call | tf_op jit(solution)/shard_map/pallas_call | solution.py:549

commit v5 on v4

--- a/solution.py
+++ b/solution.py
@@ -13,7 +13,7 @@
 PAD = 8
 LANES = 128
 WIDE = 256
-CHUNK = 1024
+CHUNK = 2048
 
 
 def advance(source, target, kappa, keep, f, starts):
@@ -160,12 +160,6 @@
     def _():
         pl.semaphore_signal(barrier, inc=1, device_id={"tile": t + 1}, device_id_type=MESH)
 
-    for mate in (core_mate, far_mate, both_mate):
-        pl.semaphore_signal(barrier, inc=1, device_id={"mem": mate}, device_id_type=MESH)
-    for d in range(1, depth):
-        mate = lax.rem(level + d, depth) * 4 + quad
-        pl.semaphore_signal(barrier, inc=1, device_id={"mem": mate}, device_id_type=MESH)
-
     loads = [
         pltpu.make_async_copy(class_hbm, classes, in_sem.at[0]),
         pltpu.make_async_copy(table_hbm, table, in_sem.at[1]),
@@ -177,8 +171,14 @@
         pltpu.make_async_copy(weights_hbm, weights, in_sem.at[7]),
         pltpu.make_async_copy(pert_hbm, pert, in_sem.at[8]),
     ]
-    for load in loads:
-        load.start()
+    for i in (0, 1, 2, 4, 3, 5, 6, 7, 8):
+        loads[i].start()
+
+    for mate in (core_mate, far_mate, both_mate):
+        pl.semaphore_signal(barrier, inc=1, device_id={"mem": mate}, device_id_type=MESH)
+    for d in range(1, depth):
+        mate = lax.rem(level + d, depth) * 4 + quad
+        pl.semaphore_signal(barrier, inc=1, device_id={"mem": mate}, device_id_type=MESH)
 
     for edge, missing in ((0, t == 0), (1, t == tiles - 1)):
 
@@ -248,6 +248,10 @@
         for j in range(lane_tiles):
             fwd0[f, j, own, :] = alpha[f, :, columns[j]]
             pack(fwd_send, f * lane_tiles + j, fwd0[f, j, top_rows, :], fwd0[f, j, bottom_rows, :])
+    pl.semaphore_wait(barrier, depth + 2 + has_up.astype(jnp.int32) + has_down.astype(jnp.int32))
+    fwd_pair = exchange(fwd_send, fwd_recv, fwd_sems)
+    start(fwd_pair)
+    static_pair = exchange(static_send, static_recv, static_sems)
     loads[3].wait()
 
     @pl.when(owner)
@@ -255,14 +259,6 @@
         for j in range(lane_tiles):
             fwd0[owned, j, own, :] = static[var, :, columns[j]]
             pack(static_send, j, fwd0[owned, j, top_rows, :], fwd0[owned, j, bottom_rows, :])
-
-    pl.semaphore_wait(barrier, depth + 2 + has_up.astype(jnp.int32) + has_down.astype(jnp.int32))
-    fwd_pair = exchange(fwd_send, fwd_recv, fwd_sems)
-    start(fwd_pair)
-    static_pair = exchange(static_send, static_recv, static_sems)
-
-    @pl.when(owner)
-    def _():
         start(static_pair)
 
     loads[4].wait()

time: 36.7 us -> 36.4 us (level)
  Pallas kernels: 35.3 us -> 34.9 us
where the time goes in v5:
time: 36.4 us; the launch traced here: 36.2 us
  Pallas kernels  34.9 us (96%)
  between operations  1.29 us (4%)
    pallas_call x1, Pallas kernels, body(): pl.pallas_call(functools.partial(kernel, tiles, members), out_shape=shape...  34.1 us
    pallas_call x1, Pallas kernels, body(): pl.pallas_call(write_out, out_shape=shapes, in_specs=[anywhere, anywhere]...  0.86 us

profile of v5, /device:TPU:4, one launch (start us, length us, event | category | flops | bytes accessed | tf_op | source)
XLA Modules:
  0.0 36.2 jit_solution(6035341385945138153)
XLA Ops:
  1.3 34.1 %shard_map.104 = (f32[3,32,768]{2,1,0:T(8,128)S(1)}, f32[4,32,768]{2,1,0:T(8,128)S(1)}) custom-call(f32[3,32,768]{2,1,0:T(8,128)} %alpha_hbm.1, f32[4,32,768]{2,1,0:T(8,128)} %static_hbm.1, bf16[3,4,32,768]{3,2,1,0:T(8,128)(2,1)} %pert_hbm.1, f32[8]{0:T(128)} %table_hbm.1, s32[32,768]{1,0:T(8,128)} %class_hbm.1, s32[32,128]{1,0:T(8,128)} %bitcast.3, ...), custom_call_target="tpu_custom_call" | custom-call | tf_op jit(solution)/shard_map/pallas_call | solution.py:492
  35.4 0.9 %shard_map.105 = (f32[3,32,768]{2,1,0:T(8,128)}, f32[4,32,768]{2,1,0:T(8,128)}) custom-call(f32[3,32,768]{2,1,0:T(8,128)S(1)} %get-tuple-element.4.alpha, f32[4,32,768]{2,1,0:T(8,128)S(1)} %get-tuple-element.5.static), custom_call_target="tpu_custom_call" | custom-call | tf_op jit(solution)/shard_map/pallas_call | solution.py:545

commit v6 on v5

--- a/solution.py
+++ b/solution.py
@@ -462,7 +462,9 @@
 
 
 def write_out(alpha, static, out_alpha, out_static, sems):
-    copies = [pltpu.make_async_copy(alpha, out_alpha, sems.at[0]), pltpu.make_async_copy(static, out_static, sems.at[1])]
+    owned = alpha.shape[0]
+    copies = [pltpu.make_async_copy(static.at[v], out_static.at[v], sems.at[owned + v]) for v in range(NVAR)]
+    copies += [pltpu.make_async_copy(alpha.at[f], out_alpha.at[f], sems.at[f]) for f in range(owned)]
     for copy in copies:
         copy.start()
     for copy in copies:
@@ -547,7 +549,7 @@
         out_shape=shapes,
         in_specs=[anywhere, anywhere],
         out_specs=(anywhere, anywhere),
-        scratch_shapes=[dma((2,))],
+        scratch_shapes=[dma((fields,))],
         compiler_params=pltpu.CompilerParams(vmem_limit_bytes=2**20),
     )(*grads)
 

time: 36.4 us -> 36.4 us (level)
  no operation moved by 1% of the time
where the time goes in v6:
time: 36.4 us; the launch traced here: 36.3 us
  Pallas kernels  35 us (96%)
  between operations  1.29 us (4%)
    pallas_call x1, Pallas kernels, body(): pl.pallas_call(functools.partial(kernel, tiles, members), out_shape=shape...  34.1 us
    pallas_call x1, Pallas kernels, body(): pl.pallas_call(write_out, out_shape=shapes, in_specs=[anywhere, anywhere]...  0.9 us

profile of v6, /device:TPU:4, one launch (start us, length us, event | category | flops | bytes accessed | tf_op | source)
XLA Modules:
  0.0 36.3 jit_solution(3230575952770064500)
XLA Ops:
  1.3 34.1 %shard_map.104 = (f32[3,32,768]{2,1,0:T(8,128)S(1)}, f32[4,32,768]{2,1,0:T(8,128)S(1)}) custom-call(f32[3,32,768]{2,1,0:T(8,128)} %alpha_hbm.1, f32[4,32,768]{2,1,0:T(8,128)} %static_hbm.1, bf16[3,4,32,768]{3,2,1,0:T(8,128)(2,1)} %pert_hbm.1, f32[8]{0:T(128)} %table_hbm.1, s32[32,768]{1,0:T(8,128)} %class_hbm.1, s32[32,128]{1,0:T(8,128)} %bitcast.3, ...), custom_call_target="tpu_custom_call" | custom-call | tf_op jit(solution)/shard_map/pallas_call | solution.py:494
  35.4 0.9 %shard_map.105 = (f32[3,32,768]{2,1,0:T(8,128)}, f32[4,32,768]{2,1,0:T(8,128)}) custom-call(f32[3,32,768]{2,1,0:T(8,128)S(1)} %get-tuple-element.4.alpha, f32[4,32,768]{2,1,0:T(8,128)S(1)} %get-tuple-element.5.static), custom_call_target="tpu_custom_call" | custom-call | tf_op jit(solution)/shard_map/pallas_call | solution.py:547
